TPU v7x, 32 devices: a whole 2x2x4 slice. The times are simulated.
32 devices in a mesh: dp: 4 (over y, core), ctx: 8 (over z, x).
Axes of the slice: x: 2, y: 2, z: 4, core: 2. Of those that a mesh axis runs over, the one named last changes fastest.
Arguments:
- queries: bfloat16 [4608, 256], P(('dp', 'ctx')), parts along dimension 0, may hold values from -5 to 5
- keys: bfloat16 [4608, 256], P(('dp', 'ctx')), parts along dimension 0, may hold values from -5 to 5
- values: bfloat16 [4608, 256], P(('dp', 'ctx')), parts along dimension 0, may hold values from -2.5 to 2.5
- out_grad: bfloat16 [4608, 256], P(('dp', 'ctx')), parts along dimension 0, may hold values from -5 to 5
- span_end: int32 [4608], P(('dp', 'ctx')), parts along dimension 0, may hold values from 0 to 1152, as said below
Outputs:
- output: bfloat16 [4608, 256], P(('dp', 'ctx')), parts along dimension 0
- query_grad: float32 [4608, 256], P(('dp', 'ctx')), parts along dimension 0
- key_grad: float32 [4608, 256], P(('dp', 'ctx')), parts along dimension 0
- value_grad: float32 [4608, 256], P(('dp', 'ctx')), parts along dimension 0
There are 4 independent parts, one for each index of `dp`. A program takes and returns all parts, laid end to end along the dimension named above; each array names one. Nothing has to cross between parts.
Inputs may be any that keep to these rules, and one draw needn't show every extreme that they name: `span_end`: image spans are runs of consecutive tokens, each of at most 288 tokens; every token of a span holds the position just past the span's last token; the last 288 tokens of a document form one span.
All inputs are finite; a program needn't handle non-finite values.
Results may differ from a plain program's by a relative error of at most 0.035.
Values may be sent and summed in bfloat16 or wider, within the bound.
A program may use at most 64 MiB of HBM per device.

v0:
```python
import functools

import jax
import jax.numpy as jnp
from jax import lax
from jax.experimental import pallas as pl
from jax.experimental.pallas import tpu as pltpu
from jax.sharding import PartitionSpec as P

HEADS = 2
HEAD_DIM = 128
IMG = 288
DIRECT = 2
HIDDEN = -1e30
KEY, VALUE, QUERY, GRAD = range(4)


def dot(a, b, a_dim, b_dim):
    return lax.dot_general(a, b, (((a_dim,), (b_dim,)), ((), ())), preferred_element_type=jnp.float32)


def kernel(
    n, rows,
    q_in, k_in, v_in, g_in, ends_in,
    o_ref, dq_ref, dk_ref, dv_ref,
    buf, ends, st, dp, st_key, dp_key, stats, top, acc_o, acc_q, acc_k, acc_v, res_out, res_in,
    send_sem, recv_sem, lim_send, lim_recv, stat_send, stat_recv, res_send, res_recv, pass_send, pass_recv,
):
    scaling = HEAD_DIM ** -0.5
    blocks = n // HEADS
    span = HEADS * rows
    cut = blocks * span - IMG
    me = lax.axis_index("ctx")
    z = me // HEADS
    x = me % HEADS
    sources = (k_in, v_in, q_in, g_in)

    def device(index):
        return {"ctx": index}

    def needed(query_block, key_block):
        return (
            (key_block <= query_block)
            | ((query_block + 1) * span > cut)
            | ((key_block <= query_block + 1) & (key_block * span < cut))
        )

    ahead = (z + 1 < blocks) & needed(z, z + 1)
    behind = (z > 0) & needed(z - 1, z)

    barrier = pltpu.get_barrier_semaphore()
    def close(target):
        return (target - z <= DIRECT) & (z - target <= DIRECT)

    met = -1
    for target in range(blocks):
        met = met + HEADS * close(target).astype(jnp.int32)
        for head in range(HEADS):
            @pl.when(close(target) & (target * HEADS + head != me))
            def _():
                pl.semaphore_signal(barrier, inc=1, device_id=device(target * HEADS + head))

    own_rows = pl.ds(pl.multiple_of(x * rows, 16), rows)
    other_rows = pl.ds(pl.multiple_of((1 - x) * rows, 16), rows)

    own_columns = pl.ds(pl.multiple_of(x * HEAD_DIM, HEAD_DIM), HEAD_DIM)
    other_columns = pl.ds(pl.multiple_of((1 - x) * HEAD_DIM, HEAD_DIM), HEAD_DIM)

    def limit_copy(slot, target, send):
        return pltpu.make_async_remote_copy(
            src_ref=ends_in, dst_ref=ends.at[slot], send_sem=lim_send.at[send],
            recv_sem=lim_recv.at[slot], device_id=device(target))

    def own_limit_copy():
        return pltpu.make_async_copy(ends_in, ends.at[x], lim_recv.at[x])

    def limits(block, slot):
        for portion in range(HEADS):
            ref = ends.at[slot + portion]
            pltpu.make_async_copy(ref, ref, lim_recv.at[slot + portion]).wait()
        joined = jnp.concatenate([ends[slot + portion] for portion in range(HEADS)], axis=1)
        position = lax.broadcasted_iota(jnp.int32, (1, span), 1) + block * span
        return jnp.maximum(position + 1, joined)

    def block_copy(array, target, head):
        return pltpu.make_async_remote_copy(
            src_ref=sources[array].at[:, pl.ds(head * HEAD_DIM, HEAD_DIM)],
            dst_ref=buf.at[array, z, own_rows],
            send_sem=send_sem.at[array, target, head],
            recv_sem=recv_sem.at[array, z, x],
            device_id=device(target * HEADS + head))

    def local_copy(array):
        return pltpu.make_async_copy(
            sources[array].at[:, own_columns],
            buf.at[array, z, own_rows],
            recv_sem.at[array, z, x])

    def stat_copy(target):
        return pltpu.make_async_remote_copy(
            src_ref=stats.at[z], dst_ref=stats.at[z], send_sem=stat_send.at[target],
            recv_sem=stat_recv.at[z], device_id=device(target * HEADS + x))

    def result_copy(slot):
        return pltpu.make_async_remote_copy(
            src_ref=res_out.at[slot], dst_ref=res_in.at[slot], send_sem=res_send.at[slot],
            recv_sem=res_recv.at[slot], device_id=device(z * HEADS + 1 - x))

    own_limit_copy().start()
    for array in range(4):
        local_copy(array).start()
    pl.semaphore_wait(barrier, met)

    limit_copy(x, z * HEADS + 1 - x, 0).start()
    @pl.when(ahead)
    def _():
        for head in range(HEADS):
            limit_copy(HEADS + x, (z + 1) * HEADS + head, 1 + head).start()

    routes = []
    order = [(array, blocks - 1 - step) for step in range(blocks) for array in (KEY, VALUE)]
    order += [(array, step) for step in range(blocks) for array in (QUERY, GRAD)]
    for array, target in order:
        wanted = needed(target, z) if array in (KEY, VALUE) else needed(z, target)
        near = close(target)
        for head in range(HEADS):
            away = target * HEADS + head != me
            routes.append((array, target, head, wanted & near & away))
    for array, target, head, wanted in routes:
        @pl.when(wanted)
        def _():
            block_copy(array, target, head).start()

    def forward_copy(array, block):
        target = z + 1 if array in (KEY, VALUE) else z - 1
        return pltpu.make_async_remote_copy(
            src_ref=buf.at[array, block], dst_ref=buf.at[array, block],
            send_sem=pass_send.at[array, block], recv_sem=pass_recv.at[array, block],
            device_id=device(target * HEADS + x))

    def forwards(array, block):
        if array in (KEY, VALUE):
            return (z - block >= DIRECT) & (z + 1 < blocks)
        return (block - z >= DIRECT) & (z > 0)

    def arrive_direct(array, block):
        for portion in range(HEADS):
            ref = buf.at[array, block, pl.ds(portion * rows, rows)]
            pltpu.make_async_copy(ref, ref, recv_sem.at[array, block, portion]).wait()

    def arrive_forwarded(array, block):
        ref = buf.at[array, block]
        pltpu.make_async_copy(ref, ref, pass_recv.at[array, block]).wait()

    def relay(arrays, block):
        @pl.when(forwards(arrays[0], block))
        def _():
            for array in arrays:
                @pl.when(close(block))
                def _():
                    arrive_direct(array, block)
                @pl.when(jnp.logical_not(close(block)))
                def _():
                    arrive_forwarded(array, block)
                forward_copy(array, block).start()

    def arrive(arrays, block):
        held = forwards(arrays[0], block)
        @pl.when(close(block) & jnp.logical_not(held))
        def _():
            for array in arrays:
                arrive_direct(array, block)
        @pl.when(jnp.logical_not(close(block) | held))
        def _():
            for array in arrays:
                arrive_forwarded(array, block)

    @pl.loop(0, blocks)
    def _(block):
        relay((KEY, VALUE), block)
        relay((QUERY, GRAD), block)

    for array in (KEY, QUERY, VALUE, GRAD):
        arrive_direct(array, z)
    own_limit = limits(z, 0)
    key_row = lax.broadcasted_iota(jnp.int32, (span, span), 0)
    top[0:1] = jnp.full((1, span), HIDDEN, jnp.float32)
    top[1:3] = jnp.zeros((2, span), jnp.float32)

    def score(block, masked):
        if not (masked == "own"):
            arrive((KEY, VALUE), block)
        scores = dot(buf[KEY, block], buf[QUERY, z], 1, 1) * scaling
        if masked:
            scores = jnp.where(key_row + block * span < own_limit, scores, HIDDEN)
        st[block] = scores
        prob_grad = dot(buf[VALUE, block], buf[GRAD, z], 1, 1)
        dp[block] = prob_grad
        highest = jnp.maximum(top[0:1], jnp.max(scores, axis=0, keepdims=True))
        probs = jnp.exp(scores - highest)
        factor = jnp.exp(top[0:1] - highest)
        top[0:1] = highest
        top[1:2] = top[1:2] * factor + jnp.sum(probs, axis=0, keepdims=True)
        top[2:3] = top[2:3] * factor + jnp.sum(probs * prob_grad, axis=0, keepdims=True)

    score(z, "own")

    @pl.when(ahead)
    def _():
        score(z + 1, "ahead")

    @pl.loop(1, z + 1)
    def _(back):
        score(z - back, None)

    log_total = top[0:1] + jnp.log(top[1:2])
    row_dot = top[2:3] / top[1:2]
    stats[z, 0:1] = log_total
    stats[z, 1:2] = row_dot
    for target in range(blocks):
        @pl.when(needed(z, target) & (z != target))
        def _():
            stat_copy(target).start()

    def own_query(block):
        probs = jnp.exp(st[block] - log_total)
        score_grad = (probs * (dp[block] - row_dot)).astype(jnp.bfloat16)
        return probs.astype(jnp.bfloat16), score_grad

    probs, score_grad = own_query(z)
    acc_o[...] = dot(probs, buf[VALUE, z], 0, 0)
    acc_q[...] = dot(score_grad, buf[KEY, z], 0, 0)
    acc_v[...] = dot(probs, buf[GRAD, z], 1, 0)
    acc_k[...] = dot(score_grad, buf[QUERY, z], 1, 0)

    def add_query(block):
        probs, score_grad = own_query(block)
        acc_o[...] += dot(probs, buf[VALUE, block], 0, 0)
        acc_q[...] += dot(score_grad, buf[KEY, block], 0, 0)

    @pl.when(ahead)
    def _():
        add_query(z + 1)

    @pl.loop(1, z + 1)
    def _(back):
        add_query(z - back)

    res_out[0] = acc_o[other_rows, :].astype(jnp.bfloat16)
    result_copy(0).start()
    res_out[1] = (acc_q[other_rows, :] * scaling).astype(jnp.bfloat16)
    result_copy(1).start()

    def key_score(block, masked):
        if masked:
            for array in (QUERY, GRAD):
                arrive_direct(array, block)
        else:
            arrive((QUERY, GRAD), block)
        scores = dot(buf[KEY, z], buf[QUERY, block], 1, 1) * scaling
        if masked:
            scores = jnp.where(key_row + z * span < limits(block, HEADS), scores, HIDDEN)
        st_key[block] = scores
        dp_key[block] = dot(buf[VALUE, z], buf[GRAD, block], 1, 1)

    @pl.when(behind)
    def _():
        key_score(z - 1, True)

    @pl.loop(z + 1, blocks)
    def _(block):
        key_score(block, False)

    def arrive_stats(block):
        pltpu.make_async_copy(stats.at[block], stats.at[block], stat_recv.at[block]).wait()

    def add_key(block, part):
        probs = jnp.exp(st_key[block, part] - stats[block, 0:1])
        acc_v[part] += dot(probs.astype(jnp.bfloat16), buf[GRAD, block], 1, 0)
        score_grad = (probs * (dp_key[block, part] - stats[block, 1:2])).astype(jnp.bfloat16)
        acc_k[part] += dot(score_grad, buf[QUERY, block], 1, 0)

    @pl.when(behind)
    def _():
        arrive_stats(z - 1)
        add_key(z - 1, slice(None))

    @pl.loop(z + 1, blocks - 1)
    def _(block):
        arrive_stats(block)
        add_key(block, slice(None))

    @pl.when(z < blocks - 1)
    def _():
        arrive_stats(blocks - 1)
        add_key(blocks - 1, other_rows)

    res_out[3] = acc_v[other_rows, :].astype(jnp.bfloat16)
    result_copy(3).start()
    res_out[2] = (acc_k[other_rows, :] * scaling).astype(jnp.bfloat16)
    result_copy(2).start()

    @pl.when(z < blocks - 1)
    def _():
        add_key(blocks - 1, own_rows)

    o_ref[:, own_columns] = acc_o[own_rows, :].astype(jnp.bfloat16)
    dq_ref[:, own_columns] = acc_q[own_rows, :] * scaling
    dk_ref[:, own_columns] = acc_k[own_rows, :] * scaling
    dv_ref[:, own_columns] = acc_v[own_rows, :]
    for slot, ref in ((0, o_ref), (1, dq_ref), (3, dv_ref), (2, dk_ref)):
        result_copy(slot).wait_recv()
        ref[:, other_columns] = res_in[slot].astype(ref.dtype)

    for slot in range(4):
        result_copy(slot).wait_send()
    limit_copy(0, 0, 0).wait_send()
    @pl.when(ahead)
    def _():
        for head in range(HEADS):
            limit_copy(0, 0, 1 + head).wait_send()
    for target in range(blocks):
        @pl.when(needed(z, target) & (z != target))
        def _():
            stat_copy(target).wait_send()
    for array, target, head, wanted in routes:
        @pl.when(wanted)
        def _():
            block_copy(array, target, head).wait_send()
    for arrays in ((KEY, VALUE), (QUERY, GRAD)):
        for block in range(blocks):
            @pl.when(forwards(arrays[0], block))
            def _():
                for array in arrays:
                    forward_copy(array, block).wait_send()


def flush(*refs):
    sem = refs[-1]
    copies = [pltpu.make_async_copy(refs[i], refs[i + 4], sem.at[i]) for i in range(4)]
    for copy in copies:
        copy.start()
    for copy in copies:
        copy.wait()


def solution(mesh):
    n = mesh.shape["ctx"]

    def local(queries, keys, values, out_grad, span_end):
        rows = queries.shape[0]
        blocks, span = n // HEADS, HEADS * rows
        f32, bf16 = jnp.float32, jnp.bfloat16
        anywhere = pl.BlockSpec(memory_space=pl.ANY)
        vmem = pl.BlockSpec(memory_space=pltpu.VMEM)
        dma = pltpu.SemaphoreType.DMA
        results = pl.pallas_call(
            functools.partial(kernel, n, rows),
            out_shape=tuple(
                pltpu.VMEM(queries.shape, kind) for kind in (bf16, f32, f32, f32)),
            in_specs=[anywhere] * 5,
            out_specs=(vmem,) * 4,
            scratch_shapes=[
                pltpu.VMEM((4, blocks, span, HEAD_DIM), bf16),
                pltpu.VMEM((2 * HEADS, 1, rows), jnp.int32),
                pltpu.VMEM((blocks, span, span), f32),
                pltpu.VMEM((blocks, span, span), f32),
                pltpu.VMEM((blocks, span, span), f32),
                pltpu.VMEM((blocks, span, span), f32),
                pltpu.VMEM((blocks, 2, span), f32),
                pltpu.VMEM((3, span), f32),
                pltpu.VMEM((span, HEAD_DIM), f32),
                pltpu.VMEM((span, HEAD_DIM), f32),
                pltpu.VMEM((span, HEAD_DIM), f32),
                pltpu.VMEM((span, HEAD_DIM), f32),
                pltpu.VMEM((4, rows, HEAD_DIM), bf16),
                pltpu.VMEM((4, rows, HEAD_DIM), bf16),
                dma((4, blocks, HEADS)),
                dma((4, blocks, HEADS)),
                dma((3,)),
                dma((2 * HEADS,)),
                dma((blocks,)),
                dma((blocks,)),
                dma((4,)),
                dma((4,)),
                dma((4, blocks)),
                dma((4, blocks)),
            ],
            compiler_params=pltpu.CompilerParams(collective_id=0, has_side_effects=True),
        )(queries, keys, values, out_grad, span_end[None])
        return pl.pallas_call(
            flush,
            out_shape=tuple(
                jax.ShapeDtypeStruct(queries.shape, kind) for kind in (bf16, f32, f32, f32)),
            in_specs=[vmem] * 4,
            out_specs=(anywhere,) * 4,
            scratch_shapes=[dma((4,))],
        )(*(pltpu.with_memory_space_constraint(result, pltpu.VMEM) for result in results))

    spec = P(("dp", "ctx"), None)
    return jax.shard_map(
        local, mesh=mesh, in_specs=(spec,) * 4 + (P(("dp", "ctx")),),
        out_specs=(spec,) * 4, check_vma=False)
```

profile of v0, /device:TPU:0, one launch (start us, length us, event | category | flops | bytes accessed | tf_op | source)
XLA Modules:
  0.0 27.6 jit_solution(16591606311169168646)
XLA Ops:
  0.6 26.2 %shard_map.84 = (bf16[144,256]{1,0:T(8,128)(2,1)S(1)}, f32[144,256]{1,0:T(8,128)S(1)}, f32[144,256]{1,0:T(8,128)S(1)}, f32[144,256]{1,0:T(8,128)S(1)}) custom-call(bf16[144,256]{1,0:T(8,128)(2,1)} %q_in.1, bf16[144,256]{1,0:T(8,128)(2,1)} %k_in.1, bf16[144,256]{1,0:T(8,128)(2,1)} %v_in.1, bf16[144,256]{1,0:T(8,128)(2,1)} %g_in.1, s32[1,144]{1,0:T(1,128)} %bitcast.1), custom_call_target="tpu_custom_call" | custom-call | tf_op jit(solution)/shard_map/pallas_call | solution.py:357
  26.8 0.8 %shard_map.85 = (bf16[144,256]{1,0:T(8,128)(2,1)}, f32[144,256]{1,0:T(8,128)}, f32[144,256]{1,0:T(8,128)}, f32[144,256]{1,0:T(8,128)}) custom-call(bf16[144,256]{1,0:T(8,128)(2,1)S(1)} %get-tuple-element.8.refs_0_, f32[144,256]{1,0:T(8,128)S(1)} %get-tuple-element.9.refs_1_, f32[144,256]{1,0:T(8,128)S(1)} %get-tuple-element.10.refs_2_, ...), custom_call_target="tpu_custom_call" | custom-call | tf_op jit(solution)/shard_map/pallas_call | solution.py:391
where the time goes:
time: 27.8 us; the launch traced here: 27.6 us
  Pallas kernels  27 us (97%)
  between operations  0.64 us (2%)
    pallas_call x1, Pallas kernels, local(): pl.pallas_call(functools.partial(kernel, n, rows), out_shape=tuple((pltpu...  26.2 us
    pallas_call x1, Pallas kernels, local(): pl.pallas_call(flush, out_shape=tuple((jax.ShapeDtypeStruct(queries.shape...  0.82 us

commit v1 on v0

v1 whole, which is shorter than its diff:
```python
import functools

import jax
import jax.numpy as jnp
from jax import lax
from jax.experimental import pallas as pl
from jax.experimental.pallas import tpu as pltpu
from jax.sharding import PartitionSpec as P

HEADS = 2
HEAD_DIM = 128
IMG = 288
HIDDEN = -1e30
KEY, VALUE, QUERY, GRAD = range(4)


def dot(a, b, a_dim, b_dim):
    return lax.dot_general(a, b, (((a_dim,), (b_dim,)), ((), ())), preferred_element_type=jnp.float32)


def kernel(
    n, rows,
    q_in, k_in, v_in, g_in, ends_in,
    o_ref, dq_ref, dk_ref, dv_ref,
    buf, ends, pe, pd, pair_stats, st_in, st_out, total, fin,
    acc_o, acc_q, acc_k, acc_v, alt, ret_out, ret_in, res_out, res_in,
    local_sem, x_recv, z_recv, end_recv, st_recv, ret_recv, res_recv, sent, ready,
):
    scaling = HEAD_DIM ** -0.5
    blocks = n // HEADS
    span = HEADS * rows
    cut = blocks * span - IMG
    last = blocks - 1
    me = lax.axis_index("ctx")
    z = me // HEADS
    x = me % HEADS
    sources = (k_in, v_in, q_in, g_in)
    OUT, DQ, DK, DV = range(4)

    def device(block, column):
        return {"ctx": block * HEADS + column}

    def ahead(block):
        return ((block + 1) * span < cut) & (block + 1 < blocks)

    def rows_of(portion):
        return pl.ds(pl.multiple_of(portion * rows, 16), rows)

    def columns_of(head):
        return pl.ds(pl.multiple_of(head * HEAD_DIM, HEAD_DIM), HEAD_DIM)

    own_rows, other_rows = rows_of(x), rows_of(1 - x)
    own_columns, other_columns = columns_of(x), columns_of(1 - x)

    key_back = span < cut
    query_back = 2 * span < cut and last > 1
    prompt = (z != 1) | (lax.axis_index("dp") % 2 == 0)
    down_key = (z == 1) & ahead(0)
    up_query = (z >= 1) & ahead(z)

    def up_key(block):
        return (z + 1 < last) | ((z + 1 == last) & (block >= 2))

    def takes_part(block, target):
        return (target >= 1) & ((target <= block) | ((target == block + 1) & ahead(block)))

    barrier = pltpu.get_barrier_semaphore()
    for target in range(1, blocks):
        @pl.when(target > z)
        def _():
            for column in range(HEADS):
                pl.semaphore_signal(barrier, inc=1, device_id=device(target, column))
    pl.semaphore_signal(barrier, inc=1, device_id=device(z, 1 - x))

    def own_copy(array):
        return pltpu.make_async_copy(
            sources[array].at[:, own_columns], buf.at[array, z, own_rows], local_sem.at[0])

    for array in range(4):
        own_copy(array).start()
    pltpu.make_async_copy(ends_in, ends.at[x], local_sem.at[1]).start()

    pl.semaphore_wait(barrier, HEADS * z + 1)
    for target in range(last):
        @pl.when(target < z)
        def _():
            for column in range(HEADS):
                pl.semaphore_signal(ready.at[z], inc=1, device_id=device(target, column))

    def remote(src, dst, recv, target, column):
        return pltpu.make_async_remote_copy(
            src_ref=src, dst_ref=dst, send_sem=sent, recv_sem=recv, device_id=device(target, column))

    def array_copy(array, block, portion, target, own=False):
        dst = buf.at[array, block, rows_of(portion)]
        return remote(
            sources[array].at[:, own_columns] if own else dst, dst,
            z_recv.at[array // 2, block], target, x)

    def query_copy(array, target, column):
        return remote(
            sources[array].at[:, columns_of(column)], buf.at[array, z, own_rows],
            z_recv.at[array // 2, z], target, column)

    def x_copy(array):
        return remote(
            sources[array].at[:, other_columns], buf.at[array, z, own_rows], x_recv.at[array], z, 1 - x)

    def x_ends():
        return remote(ends_in, ends.at[x], x_recv.at[4], z, 1 - x)

    def up_ends(column):
        return remote(ends_in, ends.at[HEADS + x], end_recv, z + 1, column)

    def landed(ref, sem):
        pltpu.make_async_copy(ref, ref, sem).wait()

    def send_query(array, portion, own):
        for target in range(last - 1, 0, -1):
            @pl.when(target < z)
            def _():
                array_copy(array, z, portion, target, own).start()

    def send_key(array, portion, own):
        @pl.when(up_key(z))
        def _():
            array_copy(array, z, portion, z + 1, own).start()

    for array in (QUERY, GRAD):
        send_query(array, x, True)
    @pl.when(down_key)
    def _():
        for array in (KEY, VALUE):
            array_copy(array, z, x, 0, True).start()
    @pl.when(z == 0)
    def _():
        for array in (KEY, VALUE, QUERY, GRAD):
            x_copy(array).start()
    @pl.when(z > 0)
    def _():
        for array in (QUERY, GRAD, KEY, VALUE):
            x_copy(array).start()
    x_ends().start()

    @pl.when(z < last)
    def _():
        pl.semaphore_wait(ready.at[z + 1], HEADS)
    for target in range(2, blocks):
        @pl.when(up_query & (target == z + 1))
        def _():
            for column in range(HEADS):
                up_ends(column).start()
            for column in (x, 1 - x):
                for array in (QUERY, GRAD):
                    query_copy(array, target, column).start()
    @pl.when(z == 0)
    def _():
        for array in (KEY, VALUE):
            send_key(array, x, True)

    def all_ready():
        @pl.loop(z + 2, blocks)
        def _(target):
            pl.semaphore_wait(ready.at[target], HEADS)

    def pass_on(array):
        landed(buf.at[array, z, other_rows], x_recv.at[array])
        if array in (KEY, VALUE):
            @pl.when(down_key)
            def _():
                array_copy(array, z, 1 - x, 0).start()
            @pl.when(prompt)
            def _():
                @pl.when(z > 0)
                def _():
                    send_key(array, x, True)
                send_key(array, 1 - x, False)
        else:
            send_query(array, 1 - x, False)

    def key_arrives(block):
        landed(buf.at[KEY:VALUE + 1, block], z_recv.at[0, block])
        @pl.when(up_key(block) & (block < z))
        def _():
            for array in (KEY, VALUE):
                for portion in range(HEADS):
                    array_copy(array, block, portion, z + 1).start()

    def query_arrives(block):
        landed(buf.at[QUERY:GRAD + 1, block], z_recv.at[1, block])

    def own_arrives():
        landed(buf.at[:, z, own_rows], local_sem.at[0])
        landed(ends.at[x], local_sem.at[1])
        landed(ends.at[1 - x], x_recv.at[4])

    def limits(block, slot):
        joined = jnp.concatenate([ends[slot + portion] for portion in range(HEADS)], axis=1)
        position = lax.broadcasted_iota(jnp.int32, (1, span), 1) + block * span
        return jnp.maximum(position + 1, joined)

    key_row = lax.broadcasted_iota(jnp.int32, (span, span), 0)

    def score(kind, slot, key_block, query_block, limit=None):
        scores = dot(buf[KEY, key_block], buf[QUERY, query_block], 1, 1) * scaling
        prob_grad = dot(buf[VALUE, key_block], buf[GRAD, query_block], 1, 1)
        if limit is not None:
            scores = jnp.where(key_row + key_block * span < limit, scores, HIDDEN)
        highest = jnp.max(scores, axis=0, keepdims=True)
        probs = jnp.exp(scores - highest)
        pe[kind, slot] = probs
        pd[kind, slot] = prob_grad
        pair_stats[kind, slot, 0:1] = highest
        pair_stats[kind, slot, 1:2] = jnp.sum(probs, axis=0, keepdims=True)
        pair_stats[kind, slot, 2:3] = jnp.sum(probs * prob_grad, axis=0, keepdims=True)

    def stat(ref):
        return ref[0:1], ref[1:2], ref[2:3]

    def pair_stat(kind, slot):
        return stat(pair_stats.at[kind, slot])

    def keep(ref, value):
        for row in range(3):
            ref[row:row + 1] = value[row]

    def merge(a, b):
        highest = jnp.maximum(a[0], b[0])
        fa, fb = jnp.exp(a[0] - highest), jnp.exp(b[0] - highest)
        return highest, a[1] * fa + b[1] * fb, a[2] * fa + b[2] * fb

    def stat_copy(block, target):
        return remote(st_out.at[block], st_in.at[z, block], st_recv.at[z - 1, block], target, x)

    def send_stat(block, value):
        keep(st_out.at[block], value)
        for target in range(1, blocks):
            @pl.when(takes_part(block, target) & (target != z))
            def _():
                stat_copy(block, target).start()

    def settle(block):
        keep(total, stat(st_out.at[block]))
        for source in range(1, blocks):
            @pl.when(takes_part(block, source) & (source != z))
            def _():
                landed(st_in.at[source, block], st_recv.at[source - 1, block])
                keep(total, merge(stat(total), stat(st_in.at[source, block])))
        finish(block, stat(total))

    def finish(block, value):
        fin[block, 0:1] = value[0] + jnp.log(value[1])
        fin[block, 1:2] = value[2] / value[1]

    def weights(kind, slot, block):
        probs = pe[kind, slot] * jnp.exp(pair_stats[kind, slot, 0:1] - fin[block, 0:1])
        score_grad = (probs * (pd[kind, slot] - fin[block, 1:2])).astype(jnp.bfloat16)
        return probs.astype(jnp.bfloat16), score_grad

    def ret_copy(slot, part, target, portion):
        return remote(
            ret_out.at[part, rows_of(portion)], ret_in.at[slot, x], ret_recv.at[slot], target, portion)

    def send_back(slot, part, target, value):
        ret_out[part] = (value * scaling if slot in (DQ, DK) else value).astype(jnp.bfloat16)
        for portion in range(HEADS):
            ret_copy(slot, part, target, portion).start()

    def res_copy(slot):
        return remote(res_out.at[slot], res_in.at[slot], res_recv.at[slot], z, 1 - x)

    def send_result(slot, acc):
        value = acc[other_rows, :]
        res_out[slot] = (value * scaling if slot in (DQ, DK) else value).astype(jnp.bfloat16)
        res_copy(slot).start()

    def emit(slot, returned):
        ref, acc = ((o_ref, acc_o), (dq_ref, acc_q), (dk_ref, acc_k), (dv_ref, acc_v))[slot]
        own = acc[own_rows, :]
        own = own * scaling if slot in (DQ, DK) else own
        res_copy(slot).wait_recv()
        other = res_in[slot].astype(jnp.float32)
        if returned:
            landed(ret_in.at[slot], ret_recv.at[slot])
            own = own + ret_in[slot, x].astype(jnp.float32)
            other = other + ret_in[slot, 1 - x].astype(jnp.float32)
        ref[:, own_columns] = own.astype(ref.dtype)
        ref[:, other_columns] = other.astype(ref.dtype)

    def key_side(kind, slot, block, into_v, into_k):
        probs, score_grad = weights(kind, slot, block)
        into_v[...] += dot(probs, buf[GRAD, block], 1, 0)
        into_k[...] += dot(score_grad, buf[QUERY, block], 1, 0)

    @pl.when(z == 0)
    def _():
        for array in (KEY, VALUE):
            pass_on(array)
        for array in (QUERY, GRAD):
            pass_on(array)
        own_arrives()
        limit = limits(0, 0)
        score(0, 0, 0, 0, limit)
        value = pair_stat(0, 0)
        if key_back:
            key_arrives(1)
            score(1, 0, 1, 0, limit)
            value = merge(value, pair_stat(1, 0))
        finish(0, value)
        probs, score_grad = weights(0, 0, 0)
        acc_o[...] = dot(probs, buf[VALUE, 0], 0, 0)
        acc_q[...] = dot(score_grad, buf[KEY, 0], 0, 0)
        acc_v[...] = dot(probs, buf[GRAD, 0], 1, 0)
        acc_k[...] = dot(score_grad, buf[QUERY, 0], 1, 0)
        if key_back:
            probs, score_grad = weights(1, 0, 0)
            send_back(DV, 0, 1, dot(probs, buf[GRAD, 0], 1, 0))
            send_back(DK, 1, 1, dot(score_grad, buf[QUERY, 0], 1, 0))
            acc_o[...] += dot(probs, buf[VALUE, 1], 0, 0)
            acc_q[...] += dot(score_grad, buf[KEY, 1], 0, 0)
        send_result(DV, acc_v)
        send_result(DK, acc_k)
        send_result(OUT, acc_o)
        send_result(DQ, acc_q)
        emit(OUT, False)
        emit(DQ, False)

    @pl.when(z == 1)
    def _():
        for array in (QUERY, GRAD, KEY, VALUE):
            pass_on(array)
        own_arrives()
        score(0, 1, 1, 1, limits(1, 0))
        @pl.when(jnp.logical_not(prompt))
        def _():
            for array in (KEY, VALUE):
                for portion in range(HEADS):
                    send_key(array, portion, False)
        key_arrives(0)
        score(1, 1, 0, 1)
        send_stat(1, merge(pair_stat(0, 1), pair_stat(1, 1)))
        all_ready()

        @pl.loop(2, blocks)
        def _(block):
            query_arrives(block)
            score(1, block, 0, block)
            score(0, block, 1, block)
            send_stat(block, merge(pair_stat(0, block), pair_stat(1, block)))

        alt[...] = jnp.zeros_like(alt)

        @pl.loop(2, last)
        def _(block):
            settle(block)
            key_side(1, block, block, alt.at[0], alt.at[1])

        settle(1)
        settle(last)
        near, near_grad = weights(1, 1, 1)
        far, far_grad = weights(1, last, last)
        ret_out[0] = (alt[0] + dot(near, buf[GRAD, 1], 1, 0) + dot(far, buf[GRAD, last], 1, 0)).astype(jnp.bfloat16)
        ret_copy(DV, 0, 0, 0).start()
        ret_out[1] = ((
            alt[1] + dot(near_grad, buf[QUERY, 1], 1, 0) + dot(far_grad, buf[QUERY, last], 1, 0)) * scaling
        ).astype(jnp.bfloat16)
        ret_copy(DK, 1, 0, 0).start()
        ret_copy(DV, 0, 0, 1).start()
        ret_copy(DK, 1, 0, 1).start()
        probs, score_grad = weights(0, last, last)
        send_back(OUT, 2, last, dot(far, buf[VALUE, 0], 0, 0) + dot(probs, buf[VALUE, 1], 0, 0))
        send_back(DQ, 3, last, dot(far_grad, buf[KEY, 0], 0, 0) + dot(score_grad, buf[KEY, 1], 0, 0))
        acc_v[...] = dot(probs, buf[GRAD, last], 1, 0)
        acc_k[...] = dot(score_grad, buf[QUERY, last], 1, 0)
        probs, score_grad = weights(0, 1, 1)
        acc_o[...] = dot(probs, buf[VALUE, 1], 0, 0) + dot(near, buf[VALUE, 0], 0, 0)
        send_result(OUT, acc_o)
        acc_q[...] = dot(score_grad, buf[KEY, 1], 0, 0) + dot(near_grad, buf[KEY, 0], 0, 0)
        send_result(DQ, acc_q)
        acc_v[...] += dot(probs, buf[GRAD, 1], 1, 0)
        acc_k[...] += dot(score_grad, buf[QUERY, 1], 1, 0)
        @pl.loop(2, last)
        def _(block):
            key_side(0, block, block, acc_v, acc_k)
        send_result(DV, acc_v)
        send_result(DK, acc_k)

    first_key = jnp.where(z == last, 2, 0)

    @pl.when(z >= 2)
    def _():
        for array in (QUERY, GRAD, KEY, VALUE):
            pass_on(array)
        own_arrives()
        score(0, z, z, z, limits(z, 0))
        send_stat(z, pair_stat(0, z))

        @pl.when(ahead(z - 1))
        def _():
            query_arrives(z - 1)
            landed(ends.at[HEADS:2 * HEADS], end_recv)
            score(0, z - 1, z, z - 1, limits(z - 1, HEADS))
            send_stat(z - 1, pair_stat(0, z - 1))

        @pl.loop(z + 1, blocks)
        def _(block):
            query_arrives(block)
            score(0, block, z, block)
            send_stat(block, pair_stat(0, block))

        all_ready()
        acc_k[...] = jnp.zeros_like(acc_k)
        acc_v[...] = jnp.zeros_like(acc_v)
        @pl.when(ahead(z - 1))
        def _():
            settle(z - 1)
            probs, score_grad = weights(0, z - 1, z - 1)
            send_back(OUT, 0, z - 1, dot(probs, buf[VALUE, z], 0, 0))
            send_back(DQ, 1, z - 1, dot(score_grad, buf[KEY, z], 0, 0))
            acc_v[...] += dot(probs, buf[GRAD, z - 1], 1, 0)
            acc_k[...] += dot(score_grad, buf[QUERY, z - 1], 1, 0)

        @pl.loop(1, z + 1 - first_key)
        def _(back):
            key_arrives(z - back)
            score(1, z - back, z - back, z)

        settle(z)
        probs, score_grad = weights(0, z, z)
        acc_o[...] = dot(probs, buf[VALUE, z], 0, 0)
        acc_q[...] = dot(score_grad, buf[KEY, z], 0, 0)
        acc_v[...] += dot(probs, buf[GRAD, z], 1, 0)
        acc_k[...] += dot(score_grad, buf[QUERY, z], 1, 0)

        @pl.loop(1, z + 1 - first_key)
        def _(back):
            block = z - back
            probs, score_grad = weights(1, block, z)
            acc_o[...] += dot(probs, buf[VALUE, block], 0, 0)
            acc_q[...] += dot(score_grad, buf[KEY, block], 0, 0)
        send_result(OUT, acc_o)
        send_result(DQ, acc_q)

        @pl.loop(z + 1, blocks)
        def _(block):
            settle(block)
            key_side(0, block, block, acc_v, acc_k)
        send_result(DV, acc_v)
        send_result(DK, acc_k)

    @pl.when(z == 0)
    def _():
        all_ready()
    for _ in range(4):
        res_copy(0).wait_send()
        x_copy(0).wait_send()
    x_ends().wait_send()
    @pl.when(up_query)
    def _():
        for column in range(HEADS):
            up_ends(column).wait_send()
            for array in (QUERY, GRAD):
                query_copy(array, z + 1, column).wait_send()
    @pl.loop(1, z)
    def _(target):
        for _ in range(4):
            array_copy(QUERY, z, 0, target).wait_send()
    @pl.when(down_key)
    def _():
        for _ in range(4):
            array_copy(KEY, z, 0, 0).wait_send()
    @pl.loop(0, z + 1)
    def _(block):
        @pl.when(up_key(block))
        def _():
            for _ in range(4):
                array_copy(KEY, block, 0, z + 1).wait_send()
    @pl.when(z >= 1)
    def _():
        @pl.loop(jnp.maximum(z - 1, 1), blocks)
        def _(block):
            @pl.when((block >= z) | ahead(z - 1))
            def _():
                for target in range(1, blocks):
                    @pl.when(takes_part(block, target) & (target != z))
                    def _():
                        stat_copy(block, target).wait_send()
    for part, wanted in ((0, ((z == 0) & ahead(0)) | (z == 1) | ((z >= 2) & ahead(z - 1))), (2, z == 1)):
        @pl.when(wanted)
        def _():
            for _ in range(4):
                ret_copy(0, part, 0, 0).wait_send()

    @pl.when(z == 0)
    def _():
        emit(DV, True)
        emit(DK, True)
    @pl.when(z == 1)
    def _():
        emit(OUT, query_back)
        emit(DQ, query_back)
        emit(DV, key_back)
        emit(DK, key_back)
    @pl.when(z >= 2)
    def _():
        returned = ahead(z) | (z == last)
        @pl.when(returned)
        def _():
            emit(OUT, True)
            emit(DQ, True)
        @pl.when(jnp.logical_not(returned))
        def _():
            emit(OUT, False)
            emit(DQ, False)
        emit(DV, False)
        emit(DK, False)


def flush(*refs):
    sem = refs[-1]
    copies = [pltpu.make_async_copy(refs[i], refs[i + 4], sem.at[i]) for i in range(4)]
    for copy in copies:
        copy.start()
    for copy in copies:
        copy.wait()


def solution(mesh):
    n = mesh.shape["ctx"]

    def local(queries, keys, values, out_grad, span_end):
        rows = queries.shape[0]
        blocks, span = n // HEADS, HEADS * rows
        f32, bf16 = jnp.float32, jnp.bfloat16
        anywhere = pl.BlockSpec(memory_space=pl.ANY)
        vmem = pl.BlockSpec(memory_space=pltpu.VMEM)
        dma = pltpu.SemaphoreType.DMA
        results = pl.pallas_call(
            functools.partial(kernel, n, rows),
            out_shape=tuple(
                pltpu.VMEM(queries.shape, kind) for kind in (bf16, f32, f32, f32)),
            in_specs=[anywhere] * 5,
            out_specs=(vmem,) * 4,
            scratch_shapes=[
                pltpu.VMEM((4, blocks, span, HEAD_DIM), bf16),
                pltpu.VMEM((2 * HEADS, 1, rows), jnp.int32),
                pltpu.VMEM((2, blocks, span, span), f32),
                pltpu.VMEM((2, blocks, span, span), f32),
                pltpu.VMEM((2, blocks, 3, span), f32),
                pltpu.VMEM((blocks, blocks, 3, span), f32),
                pltpu.VMEM((blocks, 3, span), f32),
                pltpu.VMEM((3, span), f32),
                pltpu.VMEM((blocks, 2, span), f32),
                pltpu.VMEM((span, HEAD_DIM), f32),
                pltpu.VMEM((span, HEAD_DIM), f32),
                pltpu.VMEM((span, HEAD_DIM), f32),
                pltpu.VMEM((span, HEAD_DIM), f32),
                pltpu.VMEM((2, span, HEAD_DIM), f32),
                pltpu.VMEM((4, span, HEAD_DIM), bf16),
                pltpu.VMEM((4, HEADS, rows, HEAD_DIM), bf16),
                pltpu.VMEM((4, rows, HEAD_DIM), bf16),
                pltpu.VMEM((4, rows, HEAD_DIM), bf16),
                dma((2,)),
                dma((5,)),
                dma((2, blocks)),
                dma,
                dma((blocks - 1, blocks)),
                dma((4,)),
                dma((4,)),
                dma,
                pltpu.SemaphoreType.REGULAR((blocks,)),
            ],
            compiler_params=pltpu.CompilerParams(collective_id=0, has_side_effects=True),
        )(queries, keys, values, out_grad, span_end[None])
        return pl.pallas_call(
            flush,
            out_shape=tuple(
                jax.ShapeDtypeStruct(queries.shape, kind) for kind in (bf16, f32, f32, f32)),
            in_specs=[vmem] * 4,
            out_specs=(anywhere,) * 4,
            scratch_shapes=[dma((4,))],
        )(*(pltpu.with_memory_space_constraint(result, pltpu.VMEM) for result in results))

    spec = P(("dp", "ctx"), None)
    return jax.shard_map(
        local, mesh=mesh, in_specs=(spec,) * 4 + (P(("dp", "ctx")),),
        out_specs=(spec,) * 4, check_vma=False)
```

time: 27.8 us -> 23.5 us (0.85)
  the two profiles are of different devices: /device:TPU:0 before, /device:TPU:16 now
where the time goes in v1:
time: 23.5 us; the launch traced here: 23.4 us
  Pallas kernels  22.7 us (97%)
  between operations  0.64 us (3%)
    pallas_call x1, Pallas kernels, local(): pl.pallas_call(functools.partial(kernel, n, rows), out_shape=tuple((pltpu...  21.9 us
    pallas_call x1, Pallas kernels, local(): pl.pallas_call(flush, out_shape=tuple((jax.ShapeDtypeStruct(queries.shape...  0.82 us

profile of v1, /device:TPU:16, one launch (start us, length us, event | category | flops | bytes accessed | tf_op | source)
XLA Modules:
  0.0 23.4 jit_solution(10119621756334452220)
XLA Ops:
  0.6 21.9 %shard_map.84 = (bf16[144,256]{1,0:T(8,128)(2,1)S(1)}, f32[144,256]{1,0:T(8,128)S(1)}, f32[144,256]{1,0:T(8,128)S(1)}, f32[144,256]{1,0:T(8,128)S(1)}) custom-call(bf16[144,256]{1,0:T(8,128)(2,1)} %q_in.1, bf16[144,256]{1,0:T(8,128)(2,1)} %k_in.1, bf16[144,256]{1,0:T(8,128)(2,1)} %v_in.1, bf16[144,256]{1,0:T(8,128)(2,1)} %g_in.1, s32[1,144]{1,0:T(1,128)} %bitcast.1), custom_call_target="tpu_custom_call" | custom-call | tf_op jit(solution)/shard_map/pallas_call | solution.py:538
  22.6 0.8 %shard_map.85 = (bf16[144,256]{1,0:T(8,128)(2,1)}, f32[144,256]{1,0:T(8,128)}, f32[144,256]{1,0:T(8,128)}, f32[144,256]{1,0:T(8,128)}) custom-call(bf16[144,256]{1,0:T(8,128)(2,1)S(1)} %get-tuple-element.8.refs_0_, f32[144,256]{1,0:T(8,128)S(1)} %get-tuple-element.9.refs_1_, f32[144,256]{1,0:T(8,128)S(1)} %get-tuple-element.10.refs_2_, ...), custom_call_target="tpu_custom_call" | custom-call | tf_op jit(solution)/shard_map/pallas_call | solution.py:575

commit v2 on v1

--- a/solution.py
+++ b/solution.py
@@ -54,12 +54,11 @@
 
     key_back = span < cut
     query_back = 2 * span < cut and last > 1
-    prompt = (z != 1) | (lax.axis_index("dp") % 2 == 0)
     down_key = (z == 1) & ahead(0)
     up_query = (z >= 1) & ahead(z)
 
     def up_key(block):
-        return (z + 1 < last) | ((z + 1 == last) & (block >= 2))
+        return (z < last) & ((z == 0) | (block >= 2))
 
     def takes_part(block, target):
         return (target >= 1) & ((target <= block) | ((target == block + 1) & ahead(block)))
@@ -115,23 +114,29 @@
     def landed(ref, sem):
         pltpu.make_async_copy(ref, ref, sem).wait()
 
-    def send_query(array, portion, own):
-        for target in range(last - 1, 0, -1):
-            @pl.when(target < z)
-            def _():
-                array_copy(array, z, portion, target, own).start()
+    def send_query(target):
+        for column in (x, 1 - x):
+            for array in (QUERY, GRAD):
+                query_copy(array, target, column).start()
 
     def send_key(array, portion, own):
         @pl.when(up_key(z))
         def _():
             array_copy(array, z, portion, z + 1, own).start()
 
-    for array in (QUERY, GRAD):
-        send_query(array, x, True)
+    for target in range(last - 1, 0, -1):
+        @pl.when((target < z) & (z > 2))
+        def _():
+            for array in (QUERY, GRAD):
+                query_copy(array, target, x).start()
+    @pl.when(z == 2)
+    def _():
+        send_query(1)
     @pl.when(down_key)
     def _():
-        for array in (KEY, VALUE):
-            array_copy(array, z, x, 0, True).start()
+        for column in (x, 1 - x):
+            for array in (KEY, VALUE):
+                query_copy(array, 0, column).start()
     @pl.when(z == 0)
     def _():
         for array in (KEY, VALUE, QUERY, GRAD):
@@ -150,9 +155,7 @@
         def _():
             for column in range(HEADS):
                 up_ends(column).start()
-            for column in (x, 1 - x):
-                for array in (QUERY, GRAD):
-                    query_copy(array, target, column).start()
+            send_query(target)
     @pl.when(z == 0)
     def _():
         for array in (KEY, VALUE):
@@ -166,17 +169,16 @@
     def pass_on(array):
         landed(buf.at[array, z, other_rows], x_recv.at[array])
         if array in (KEY, VALUE):
-            @pl.when(down_key)
+            @pl.when(z > 0)
             def _():
-                array_copy(array, z, 1 - x, 0).start()
-            @pl.when(prompt)
-            def _():
-                @pl.when(z > 0)
+                send_key(array, x, True)
+            send_key(array, 1 - x, False)
+        elif array == GRAD:
+            for target in range(last - 1, 0, -1):
+                @pl.when((target < z) & (z > 2))
                 def _():
-                    send_key(array, x, True)
-                send_key(array, 1 - x, False)
-        else:
-            send_query(array, 1 - x, False)
+                    for half in (QUERY, GRAD):
+                        array_copy(half, z, 1 - x, target).start()
 
     def key_arrives(block):
         landed(buf.at[KEY:VALUE + 1, block], z_recv.at[0, block])
@@ -257,14 +259,15 @@
         score_grad = (probs * (pd[kind, slot] - fin[block, 1:2])).astype(jnp.bfloat16)
         return probs.astype(jnp.bfloat16), score_grad
 
-    def ret_copy(slot, part, target, portion):
+    def ret_copy(origin, slot, part, target, portion):
         return remote(
-            ret_out.at[part, rows_of(portion)], ret_in.at[slot, x], ret_recv.at[slot], target, portion)
-
-    def send_back(slot, part, target, value):
+            ret_out.at[part, rows_of(portion)], ret_in.at[origin, slot, x], ret_recv.at[origin, slot],
+            target, portion)
+
+    def send_back(origin, slot, part, target, value):
         ret_out[part] = (value * scaling if slot in (DQ, DK) else value).astype(jnp.bfloat16)
         for portion in range(HEADS):
-            ret_copy(slot, part, target, portion).start()
+            ret_copy(origin, slot, part, target, portion).start()
 
     def res_copy(slot):
         return remote(res_out.at[slot], res_in.at[slot], res_recv.at[slot], z, 1 - x)
@@ -274,16 +277,18 @@
         res_out[slot] = (value * scaling if slot in (DQ, DK) else value).astype(jnp.bfloat16)
         res_copy(slot).start()
 
-    def emit(slot, returned):
+    HUB, SIDE = range(2)
+
+    def emit(slot, *origins):
         ref, acc = ((o_ref, acc_o), (dq_ref, acc_q), (dk_ref, acc_k), (dv_ref, acc_v))[slot]
         own = acc[own_rows, :]
         own = own * scaling if slot in (DQ, DK) else own
         res_copy(slot).wait_recv()
         other = res_in[slot].astype(jnp.float32)
-        if returned:
-            landed(ret_in.at[slot], ret_recv.at[slot])
-            own = own + ret_in[slot, x].astype(jnp.float32)
-            other = other + ret_in[slot, 1 - x].astype(jnp.float32)
+        for origin in origins:
+            landed(ret_in.at[origin, slot], ret_recv.at[origin, slot])
+            own = own + ret_in[origin, slot, x].astype(jnp.float32)
+            other = other + ret_in[origin, slot, 1 - x].astype(jnp.float32)
         ref[:, own_columns] = own.astype(ref.dtype)
         ref[:, other_columns] = other.astype(ref.dtype)
 
@@ -314,16 +319,16 @@
         acc_k[...] = dot(score_grad, buf[QUERY, 0], 1, 0)
         if key_back:
             probs, score_grad = weights(1, 0, 0)
-            send_back(DV, 0, 1, dot(probs, buf[GRAD, 0], 1, 0))
-            send_back(DK, 1, 1, dot(score_grad, buf[QUERY, 0], 1, 0))
+            send_back(SIDE, DV, 0, 1, dot(probs, buf[GRAD, 0], 1, 0))
+            send_back(SIDE, DK, 1, 1, dot(score_grad, buf[QUERY, 0], 1, 0))
             acc_o[...] += dot(probs, buf[VALUE, 1], 0, 0)
             acc_q[...] += dot(score_grad, buf[KEY, 1], 0, 0)
         send_result(DV, acc_v)
         send_result(DK, acc_k)
         send_result(OUT, acc_o)
         send_result(DQ, acc_q)
-        emit(OUT, False)
-        emit(DQ, False)
+        emit(OUT)
+        emit(DQ)
 
     @pl.when(z == 1)
     def _():
@@ -331,61 +336,68 @@
             pass_on(array)
         own_arrives()
         score(0, 1, 1, 1, limits(1, 0))
-        @pl.when(jnp.logical_not(prompt))
-        def _():
-            for array in (KEY, VALUE):
-                for portion in range(HEADS):
-                    send_key(array, portion, False)
         key_arrives(0)
         score(1, 1, 0, 1)
         send_stat(1, merge(pair_stat(0, 1), pair_stat(1, 1)))
         all_ready()
 
-        @pl.loop(2, blocks)
-        def _(block):
+        def scores_of(block):
             query_arrives(block)
             score(1, block, 0, block)
             score(0, block, 1, block)
             send_stat(block, merge(pair_stat(0, block), pair_stat(1, block)))
 
+        def query_side(far, far_grad, near, near_grad):
+            return (
+                dot(far, buf[VALUE, 0], 0, 0) + dot(near, buf[VALUE, 1], 0, 0),
+                dot(far_grad, buf[KEY, 0], 0, 0) + dot(near_grad, buf[KEY, 1], 0, 0))
+
         alt[...] = jnp.zeros_like(alt)
+
+        @pl.loop(2, blocks)
+        def _(block):
+            scores_of(block)
 
         @pl.loop(2, last)
         def _(block):
             settle(block)
             key_side(1, block, block, alt.at[0], alt.at[1])
-
         settle(1)
+        key_side(1, 1, 1, alt.at[0], alt.at[1])
         settle(last)
-        near, near_grad = weights(1, 1, 1)
         far, far_grad = weights(1, last, last)
-        ret_out[0] = (alt[0] + dot(near, buf[GRAD, 1], 1, 0) + dot(far, buf[GRAD, last], 1, 0)).astype(jnp.bfloat16)
-        ret_copy(DV, 0, 0, 0).start()
-        ret_out[1] = ((
-            alt[1] + dot(near_grad, buf[QUERY, 1], 1, 0) + dot(far_grad, buf[QUERY, last], 1, 0)) * scaling
-        ).astype(jnp.bfloat16)
-        ret_copy(DK, 1, 0, 0).start()
-        ret_copy(DV, 0, 0, 1).start()
-        ret_copy(DK, 1, 0, 1).start()
-        probs, score_grad = weights(0, last, last)
-        send_back(OUT, 2, last, dot(far, buf[VALUE, 0], 0, 0) + dot(probs, buf[VALUE, 1], 0, 0))
-        send_back(DQ, 3, last, dot(far_grad, buf[KEY, 0], 0, 0) + dot(score_grad, buf[KEY, 1], 0, 0))
-        acc_v[...] = dot(probs, buf[GRAD, last], 1, 0)
-        acc_k[...] = dot(score_grad, buf[QUERY, last], 1, 0)
-        probs, score_grad = weights(0, 1, 1)
-        acc_o[...] = dot(probs, buf[VALUE, 1], 0, 0) + dot(near, buf[VALUE, 0], 0, 0)
+        ret_out[0] = (alt[0] + dot(far, buf[GRAD, last], 1, 0)).astype(jnp.bfloat16)
+        ret_copy(HUB, DV, 0, 0, 0).start()
+        ret_out[1] = ((alt[1] + dot(far_grad, buf[QUERY, last], 1, 0)) * scaling).astype(jnp.bfloat16)
+        ret_copy(HUB, DK, 1, 0, 0).start()
+        ret_copy(HUB, DV, 0, 0, 1).start()
+        ret_copy(HUB, DK, 1, 0, 1).start()
+        near, near_grad = weights(0, last, last)
+        output, query_grad = query_side(far, far_grad, near, near_grad)
+        send_back(HUB, OUT, 2 * last, last, output)
+        send_back(HUB, DQ, 2 * last + 1, last, query_grad)
+        acc_v[...] = dot(near, buf[GRAD, last], 1, 0)
+        acc_k[...] = dot(near_grad, buf[QUERY, last], 1, 0)
+
+        far, far_grad = weights(1, 1, 1)
+        near, near_grad = weights(0, 1, 1)
+        acc_o[...], acc_q[...] = query_side(far, far_grad, near, near_grad)
         send_result(OUT, acc_o)
-        acc_q[...] = dot(score_grad, buf[KEY, 1], 0, 0) + dot(near_grad, buf[KEY, 0], 0, 0)
         send_result(DQ, acc_q)
-        acc_v[...] += dot(probs, buf[GRAD, 1], 1, 0)
-        acc_k[...] += dot(score_grad, buf[QUERY, 1], 1, 0)
+        acc_v[...] += dot(near, buf[GRAD, 1], 1, 0)
+        acc_k[...] += dot(near_grad, buf[QUERY, 1], 1, 0)
+
         @pl.loop(2, last)
         def _(block):
-            key_side(0, block, block, acc_v, acc_k)
+            far, far_grad = weights(1, block, block)
+            near, near_grad = weights(0, block, block)
+            acc_v[...] += dot(near, buf[GRAD, block], 1, 0)
+            acc_k[...] += dot(near_grad, buf[QUERY, block], 1, 0)
+            output, query_grad = query_side(far, far_grad, near, near_grad)
+            send_back(HUB, OUT, 2 * block, block, output)
+            send_back(HUB, DQ, 2 * block + 1, block, query_grad)
         send_result(DV, acc_v)
         send_result(DK, acc_k)
-
-    first_key = jnp.where(z == last, 2, 0)
 
     @pl.when(z >= 2)
     def _():
@@ -415,24 +427,28 @@
         def _():
             settle(z - 1)
             probs, score_grad = weights(0, z - 1, z - 1)
-            send_back(OUT, 0, z - 1, dot(probs, buf[VALUE, z], 0, 0))
-            send_back(DQ, 1, z - 1, dot(score_grad, buf[KEY, z], 0, 0))
+            send_back(SIDE, OUT, 0, z - 1, dot(probs, buf[VALUE, z], 0, 0))
+            send_back(SIDE, DQ, 1, z - 1, dot(score_grad, buf[KEY, z], 0, 0))
             acc_v[...] += dot(probs, buf[GRAD, z - 1], 1, 0)
             acc_k[...] += dot(score_grad, buf[QUERY, z - 1], 1, 0)
 
-        @pl.loop(1, z + 1 - first_key)
+        @pl.loop(1, z - 1)
         def _(back):
             key_arrives(z - back)
             score(1, z - back, z - back, z)
 
         settle(z)
         probs, score_grad = weights(0, z, z)
+        acc_v[...] += dot(probs, buf[GRAD, z], 1, 0)
+        acc_k[...] += dot(score_grad, buf[QUERY, z], 1, 0)
+        @pl.when(z == last)
+        def _():
+            send_result(DV, acc_v)
+            send_result(DK, acc_k)
         acc_o[...] = dot(probs, buf[VALUE, z], 0, 0)
         acc_q[...] = dot(score_grad, buf[KEY, z], 0, 0)
-        acc_v[...] += dot(probs, buf[GRAD, z], 1, 0)
-        acc_k[...] += dot(score_grad, buf[QUERY, z], 1, 0)
-
-        @pl.loop(1, z + 1 - first_key)
+
+        @pl.loop(1, z - 1)
         def _(back):
             block = z - back
             probs, score_grad = weights(1, block, z)
@@ -441,12 +457,14 @@
         send_result(OUT, acc_o)
         send_result(DQ, acc_q)
 
-        @pl.loop(z + 1, blocks)
-        def _(block):
-            settle(block)
-            key_side(0, block, block, acc_v, acc_k)
-        send_result(DV, acc_v)
-        send_result(DK, acc_k)
+        @pl.when(z < last)
+        def _():
+            @pl.loop(z + 1, blocks)
+            def _(block):
+                settle(block)
+                key_side(0, block, block, acc_v, acc_k)
+            send_result(DV, acc_v)
+            send_result(DK, acc_k)
 
     @pl.when(z == 0)
     def _():
@@ -464,11 +482,11 @@
     @pl.loop(1, z)
     def _(target):
         for _ in range(4):
-            array_copy(QUERY, z, 0, target).wait_send()
+            query_copy(QUERY, target, x).wait_send()
     @pl.when(down_key)
     def _():
         for _ in range(4):
-            array_copy(KEY, z, 0, 0).wait_send()
+            query_copy(KEY, 0, x).wait_send()
     @pl.loop(0, z + 1)
     def _(block):
         @pl.when(up_key(block))
@@ -485,35 +503,39 @@
                     @pl.when(takes_part(block, target) & (target != z))
                     def _():
                         stat_copy(block, target).wait_send()
-    for part, wanted in ((0, ((z == 0) & ahead(0)) | (z == 1) | ((z >= 2) & ahead(z - 1))), (2, z == 1)):
-        @pl.when(wanted)
-        def _():
+    @pl.when(((z == 0) & ahead(0)) | (z == 1) | ((z >= 2) & ahead(z - 1)))
+    def _():
+        for _ in range(4):
+            ret_copy(HUB, OUT, 0, 0, 0).wait_send()
+    @pl.when(z == 1)
+    def _():
+        @pl.loop(2, blocks)
+        def _(block):
             for _ in range(4):
-                ret_copy(0, part, 0, 0).wait_send()
+                ret_copy(HUB, OUT, 0, 0, 0).wait_send()
 
     @pl.when(z == 0)
     def _():
-        emit(DV, True)
-        emit(DK, True)
+        emit(DV, HUB)
+        emit(DK, HUB)
     @pl.when(z == 1)
     def _():
-        emit(OUT, query_back)
-        emit(DQ, query_back)
-        emit(DV, key_back)
-        emit(DK, key_back)
+        for slot in (OUT, DQ):
+            emit(slot, *((SIDE,) if query_back else ()))
+        for slot in (DV, DK):
+            emit(slot, *((SIDE,) if key_back else ()))
     @pl.when(z >= 2)
     def _():
-        returned = ahead(z) | (z == last)
-        @pl.when(returned)
-        def _():
-            emit(OUT, True)
-            emit(DQ, True)
-        @pl.when(jnp.logical_not(returned))
-        def _():
-            emit(OUT, False)
-            emit(DQ, False)
-        emit(DV, False)
-        emit(DK, False)
+        @pl.when(ahead(z))
+        def _():
+            emit(OUT, HUB, SIDE)
+            emit(DQ, HUB, SIDE)
+        @pl.when(jnp.logical_not(ahead(z)))
+        def _():
+            emit(OUT, HUB)
+            emit(DQ, HUB)
+        emit(DV)
+        emit(DK)
 
 
 def flush(*refs):
@@ -556,8 +578,8 @@
                 pltpu.VMEM((span, HEAD_DIM), f32),
                 pltpu.VMEM((span, HEAD_DIM), f32),
                 pltpu.VMEM((2, span, HEAD_DIM), f32),
-                pltpu.VMEM((4, span, HEAD_DIM), bf16),
-                pltpu.VMEM((4, HEADS, rows, HEAD_DIM), bf16),
+                pltpu.VMEM((2 * blocks, span, HEAD_DIM), bf16),
+                pltpu.VMEM((2, 4, HEADS, rows, HEAD_DIM), bf16),
                 pltpu.VMEM((4, rows, HEAD_DIM), bf16),
                 pltpu.VMEM((4, rows, HEAD_DIM), bf16),
                 dma((2,)),
@@ -565,7 +587,7 @@
                 dma((2, blocks)),
                 dma,
                 dma((blocks - 1, blocks)),
-                dma((4,)),
+                dma((2, 4)),
                 dma((4,)),
                 dma,
                 pltpu.SemaphoreType.REGULAR((blocks,)),

time: 23.5 us -> 21.4 us (0.911)
  the two profiles are of different devices: /device:TPU:16 before, /device:TPU:0 now
where the time goes in v2:
time: 21.4 us; the launch traced here: 21.1 us
  Pallas kernels  20.4 us (95%)
  between operations  0.64 us (3%)
    pallas_call x1, Pallas kernels, local(): pl.pallas_call(functools.partial(kernel, n, rows), out_shape=tuple((pltpu...  19.6 us
    pallas_call x1, Pallas kernels, local(): pl.pallas_call(flush, out_shape=tuple((jax.ShapeDtypeStruct(queries.shape...  0.82 us

profile of v2, /device:TPU:0, one launch (start us, length us, event | category | flops | bytes accessed | tf_op | source)
XLA Modules:
  0.0 21.1 jit_solution(10778967960726341574)
XLA Ops:
  0.6 19.6 %shard_map.84 = (bf16[144,256]{1,0:T(8,128)(2,1)S(1)}, f32[144,256]{1,0:T(8,128)S(1)}, f32[144,256]{1,0:T(8,128)S(1)}, f32[144,256]{1,0:T(8,128)S(1)}) custom-call(bf16[144,256]{1,0:T(8,128)(2,1)} %q_in.1, bf16[144,256]{1,0:T(8,128)(2,1)} %k_in.1, bf16[144,256]{1,0:T(8,128)(2,1)} %v_in.1, bf16[144,256]{1,0:T(8,128)(2,1)} %g_in.1, s32[1,144]{1,0:T(1,128)} %bitcast.1), custom_call_target="tpu_custom_call" | custom-call | tf_op jit(solution)/shard_map/pallas_call | solution.py:560
  20.3 0.8 %shard_map.85 = (bf16[144,256]{1,0:T(8,128)(2,1)}, f32[144,256]{1,0:T(8,128)}, f32[144,256]{1,0:T(8,128)}, f32[144,256]{1,0:T(8,128)}) custom-call(bf16[144,256]{1,0:T(8,128)(2,1)S(1)} %get-tuple-element.8.refs_0_, f32[144,256]{1,0:T(8,128)S(1)} %get-tuple-element.9.refs_1_, f32[144,256]{1,0:T(8,128)S(1)} %get-tuple-element.10.refs_2_, ...), custom_call_target="tpu_custom_call" | custom-call | tf_op jit(solution)/shard_map/pallas_call | solution.py:597

commit v3 on v2

--- a/solution.py
+++ b/solution.py
@@ -84,7 +84,7 @@
         @pl.when(target < z)
         def _():
             for column in range(HEADS):
-                pl.semaphore_signal(ready.at[z], inc=1, device_id=device(target, column))
+                pl.semaphore_signal(ready.at[z - 1], inc=1, device_id=device(target, column))
 
     def remote(src, dst, recv, target, column):
         return pltpu.make_async_remote_copy(
@@ -124,6 +124,14 @@
         def _():
             array_copy(array, z, portion, z + 1, own).start()
 
+    @pl.when(z == 0)
+    def _():
+        for array in (KEY, VALUE, QUERY, GRAD):
+            x_copy(array).start()
+    @pl.when(z > 0)
+    def _():
+        for array in (QUERY, GRAD, KEY, VALUE):
+            x_copy(array).start()
     for target in range(last - 1, 0, -1):
         @pl.when((target < z) & (z > 2))
         def _():
@@ -137,19 +145,11 @@
         for column in (x, 1 - x):
             for array in (KEY, VALUE):
                 query_copy(array, 0, column).start()
-    @pl.when(z == 0)
-    def _():
-        for array in (KEY, VALUE, QUERY, GRAD):
-            x_copy(array).start()
-    @pl.when(z > 0)
-    def _():
-        for array in (QUERY, GRAD, KEY, VALUE):
-            x_copy(array).start()
     x_ends().start()
 
     @pl.when(z < last)
     def _():
-        pl.semaphore_wait(ready.at[z + 1], HEADS)
+        pl.semaphore_wait(ready.at[z], HEADS)
     for target in range(2, blocks):
         @pl.when(up_query & (target == z + 1))
         def _():
@@ -164,7 +164,7 @@
     def all_ready():
         @pl.loop(z + 2, blocks)
         def _(target):
-            pl.semaphore_wait(ready.at[target], HEADS)
+            pl.semaphore_wait(ready.at[target - 1], HEADS)
 
     def pass_on(array):
         landed(buf.at[array, z, other_rows], x_recv.at[array])
@@ -173,12 +173,16 @@
             def _():
                 send_key(array, x, True)
             send_key(array, 1 - x, False)
-        elif array == GRAD:
-            for target in range(last - 1, 0, -1):
-                @pl.when((target < z) & (z > 2))
-                def _():
-                    for half in (QUERY, GRAD):
-                        array_copy(half, z, 1 - x, target).start()
+        else:
+            @pl.when(z > 2)
+            def _():
+                array_copy(array, z, 1 - x, z - 1).start()
+                if array == GRAD:
+                    for target in range(last - 2, 0, -1):
+                        @pl.when(target < z - 1)
+                        def _():
+                            for half in (QUERY, GRAD):
+                                array_copy(half, z, 1 - x, target).start()
 
     def key_arrives(block):
         landed(buf.at[KEY:VALUE + 1, block], z_recv.at[0, block])
@@ -232,7 +236,7 @@
         return highest, a[1] * fa + b[1] * fb, a[2] * fa + b[2] * fb
 
     def stat_copy(block, target):
-        return remote(st_out.at[block], st_in.at[z, block], st_recv.at[z - 1, block], target, x)
+        return remote(st_out.at[block], st_in.at[z, block], st_recv.at[z - 1, block - 1], target, x)
 
     def send_stat(block, value):
         keep(st_out.at[block], value)
@@ -246,7 +250,7 @@
         for source in range(1, blocks):
             @pl.when(takes_part(block, source) & (source != z))
             def _():
-                landed(st_in.at[source, block], st_recv.at[source - 1, block])
+                landed(st_in.at[source, block], st_recv.at[source - 1, block - 1])
                 keep(total, merge(stat(total), stat(st_in.at[source, block])))
         finish(block, stat(total))
 
@@ -361,7 +365,13 @@
         @pl.loop(2, last)
         def _(block):
             settle(block)
-            key_side(1, block, block, alt.at[0], alt.at[1])
+            far, far_grad = weights(1, block, block)
+            alt[0] += dot(far, buf[GRAD, block], 1, 0)
+            alt[1] += dot(far_grad, buf[QUERY, block], 1, 0)
+            near, near_grad = weights(0, block, block)
+            output, query_grad = query_side(far, far_grad, near, near_grad)
+            send_back(HUB, OUT, 2 * block, block, output)
+            send_back(HUB, DQ, 2 * block + 1, block, query_grad)
         settle(1)
         key_side(1, 1, 1, alt.at[0], alt.at[1])
         settle(last)
@@ -389,13 +399,7 @@
 
         @pl.loop(2, last)
         def _(block):
-            far, far_grad = weights(1, block, block)
-            near, near_grad = weights(0, block, block)
-            acc_v[...] += dot(near, buf[GRAD, block], 1, 0)
-            acc_k[...] += dot(near_grad, buf[QUERY, block], 1, 0)
-            output, query_grad = query_side(far, far_grad, near, near_grad)
-            send_back(HUB, OUT, 2 * block, block, output)
-            send_back(HUB, DQ, 2 * block + 1, block, query_grad)
+            key_side(0, block, block, acc_v, acc_k)
         send_result(DV, acc_v)
         send_result(DK, acc_k)
 
@@ -586,11 +590,11 @@
                 dma((5,)),
                 dma((2, blocks)),
                 dma,
-                dma((blocks - 1, blocks)),
+                dma((blocks - 1, blocks - 1)),
                 dma((2, 4)),
                 dma((4,)),
                 dma,
-                pltpu.SemaphoreType.REGULAR((blocks,)),
+                pltpu.SemaphoreType.REGULAR((blocks - 1,)),
             ],
             compiler_params=pltpu.CompilerParams(collective_id=0, has_side_effects=True),
         )(queries, keys, values, out_grad, span_end[None])

time: 21.4 us -> 20.9 us (0.977)
  Pallas kernels: 20.4 us -> 20 us
    pallas_call x1, Pallas kernels: 19.6 us -> 19.2 us  [local(): pl.pallas_call(functools.partial(kernel, n, rows), out_shape=tuple((pltpu...]
where the time goes in v3:
time: 20.9 us; the launch traced here: 20.6 us
  Pallas kernels  20 us (96%)
  between operations  0.64 us (3%)
    pallas_call x1, Pallas kernels, local(): pl.pallas_call(functools.partial(kernel, n, rows), out_shape=tuple((pltpu...  19.2 us
    pallas_call x1, Pallas kernels, local(): pl.pallas_call(flush, out_shape=tuple((jax.ShapeDtypeStruct(queries.shape...  0.82 us

profile of v3, /device:TPU:0, one launch (start us, length us, event | category | flops | bytes accessed | tf_op | source)
XLA Modules:
  0.0 20.6 jit_solution(18412545099856061698)
XLA Ops:
  0.6 19.2 %shard_map.84 = (bf16[144,256]{1,0:T(8,128)(2,1)S(1)}, f32[144,256]{1,0:T(8,128)S(1)}, f32[144,256]{1,0:T(8,128)S(1)}, f32[144,256]{1,0:T(8,128)S(1)}) custom-call(bf16[144,256]{1,0:T(8,128)(2,1)} %q_in.1, bf16[144,256]{1,0:T(8,128)(2,1)} %k_in.1, bf16[144,256]{1,0:T(8,128)(2,1)} %v_in.1, bf16[144,256]{1,0:T(8,128)(2,1)} %g_in.1, s32[1,144]{1,0:T(1,128)} %bitcast.1), custom_call_target="tpu_custom_call" | custom-call | tf_op jit(solution)/shard_map/pallas_call | solution.py:564
  19.8 0.8 %shard_map.85 = (bf16[144,256]{1,0:T(8,128)(2,1)}, f32[144,256]{1,0:T(8,128)}, f32[144,256]{1,0:T(8,128)}, f32[144,256]{1,0:T(8,128)}) custom-call(bf16[144,256]{1,0:T(8,128)(2,1)S(1)} %get-tuple-element.8.refs_0_, f32[144,256]{1,0:T(8,128)S(1)} %get-tuple-element.9.refs_1_, f32[144,256]{1,0:T(8,128)S(1)} %get-tuple-element.10.refs_2_, ...), custom_call_target="tpu_custom_call" | custom-call | tf_op jit(solution)/shard_map/pallas_call | solution.py:601

commit v4 on v3

--- a/solution.py
+++ b/solution.py
@@ -155,7 +155,8 @@
         def _():
             for column in range(HEADS):
                 up_ends(column).start()
-            send_query(target)
+            for array in (QUERY, GRAD):
+                query_copy(array, target, x).start()
     @pl.when(z == 0)
     def _():
         for array in (KEY, VALUE):
@@ -174,6 +175,9 @@
                 send_key(array, x, True)
             send_key(array, 1 - x, False)
         else:
+            @pl.when(up_query)
+            def _():
+                array_copy(array, z, 1 - x, z + 1).start()
             @pl.when(z > 2)
             def _():
                 array_copy(array, z, 1 - x, z - 1).start()
@@ -268,8 +272,11 @@
             ret_out.at[part, rows_of(portion)], ret_in.at[origin, slot, x], ret_recv.at[origin, slot],
             target, portion)
 
+    def hold_back(slot, part, value):
+        ret_out[part] = (value * scaling if slot in (DQ, DK) else value).astype(jnp.bfloat16)
+
     def send_back(origin, slot, part, target, value):
-        ret_out[part] = (value * scaling if slot in (DQ, DK) else value).astype(jnp.bfloat16)
+        hold_back(slot, part, value)
         for portion in range(HEADS):
             ret_copy(origin, slot, part, target, portion).start()
 
@@ -358,20 +365,26 @@
 
         alt[...] = jnp.zeros_like(alt)
 
-        @pl.loop(2, blocks)
-        def _(block):
-            scores_of(block)
-
-        @pl.loop(2, last)
-        def _(block):
+        alt[...] = jnp.zeros_like(alt)
+
+        def finish_block(block):
             settle(block)
             far, far_grad = weights(1, block, block)
             alt[0] += dot(far, buf[GRAD, block], 1, 0)
             alt[1] += dot(far_grad, buf[QUERY, block], 1, 0)
             near, near_grad = weights(0, block, block)
             output, query_grad = query_side(far, far_grad, near, near_grad)
-            send_back(HUB, OUT, 2 * block, block, output)
-            send_back(HUB, DQ, 2 * block + 1, block, query_grad)
+            hold_back(OUT, 2 * block, output)
+            hold_back(DQ, 2 * block + 1, query_grad)
+
+        pl.loop(2, last)(scores_of)
+        pl.loop(2, last)(finish_block)
+        scores_of(last)
+        @pl.loop(2, last)
+        def _(block):
+            for part, slot in enumerate((OUT, DQ)):
+                for portion in range(HEADS):
+                    ret_copy(HUB, slot, 2 * block + part, block, portion).start()
         settle(1)
         key_side(1, 1, 1, alt.at[0], alt.at[1])
         settle(last)

time: 20.9 us -> 20.8 us (level)
  no operation moved by 1% of the time
where the time goes in v4:
time: 20.8 us; the launch traced here: 20.6 us
  Pallas kernels  20 us (96%)
  between operations  0.64 us (3%)
    pallas_call x1, Pallas kernels, local(): pl.pallas_call(functools.partial(kernel, n, rows), out_shape=tuple((pltpu...  19.2 us
    pallas_call x1, Pallas kernels, local(): pl.pallas_call(flush, out_shape=tuple((jax.ShapeDtypeStruct(queries.shape...  0.82 us

profile of v4, /device:TPU:0, one launch (start us, length us, event | category | flops | bytes accessed | tf_op | source)
XLA Modules:
  0.0 20.6 jit_solution(6062799578962889979)
XLA Ops:
  0.6 19.2 %shard_map.84 = (bf16[144,256]{1,0:T(8,128)(2,1)S(1)}, f32[144,256]{1,0:T(8,128)S(1)}, f32[144,256]{1,0:T(8,128)S(1)}, f32[144,256]{1,0:T(8,128)S(1)}) custom-call(bf16[144,256]{1,0:T(8,128)(2,1)} %q_in.1, bf16[144,256]{1,0:T(8,128)(2,1)} %k_in.1, bf16[144,256]{1,0:T(8,128)(2,1)} %v_in.1, bf16[144,256]{1,0:T(8,128)(2,1)} %g_in.1, s32[1,144]{1,0:T(1,128)} %bitcast.1), custom_call_target="tpu_custom_call" | custom-call | tf_op jit(solution)/shard_map/pallas_call | solution.py:577
  19.8 0.8 %shard_map.85 = (bf16[144,256]{1,0:T(8,128)(2,1)}, f32[144,256]{1,0:T(8,128)}, f32[144,256]{1,0:T(8,128)}, f32[144,256]{1,0:T(8,128)}) custom-call(bf16[144,256]{1,0:T(8,128)(2,1)S(1)} %get-tuple-element.8.refs_0_, f32[144,256]{1,0:T(8,128)S(1)} %get-tuple-element.9.refs_1_, f32[144,256]{1,0:T(8,128)S(1)} %get-tuple-element.10.refs_2_, ...), custom_call_target="tpu_custom_call" | custom-call | tf_op jit(solution)/shard_map/pallas_call | solution.py:614

commit v5 on v4

--- a/solution.py
+++ b/solution.py
@@ -1,4 +1,5 @@
 import functools
+import math
 
 import jax
 import jax.numpy as jnp
@@ -27,6 +28,7 @@
     local_sem, x_recv, z_recv, end_recv, st_recv, ret_recv, res_recv, sent, ready,
 ):
     scaling = HEAD_DIM ** -0.5
+    binary = scaling / math.log(2.0)
     blocks = n // HEADS
     span = HEADS * rows
     cut = blocks * span - IMG
@@ -212,15 +214,15 @@
     key_row = lax.broadcasted_iota(jnp.int32, (span, span), 0)
 
     def score(kind, slot, key_block, query_block, limit=None):
-        scores = dot(buf[KEY, key_block], buf[QUERY, query_block], 1, 1) * scaling
+        scores = dot(buf[KEY, key_block], buf[QUERY, query_block], 1, 1)
         prob_grad = dot(buf[VALUE, key_block], buf[GRAD, query_block], 1, 1)
         if limit is not None:
             scores = jnp.where(key_row + key_block * span < limit, scores, HIDDEN)
         highest = jnp.max(scores, axis=0, keepdims=True)
-        probs = jnp.exp(scores - highest)
+        probs = jnp.exp2((scores - highest) * binary)
         pe[kind, slot] = probs
         pd[kind, slot] = prob_grad
-        pair_stats[kind, slot, 0:1] = highest
+        pair_stats[kind, slot, 0:1] = highest * binary
         pair_stats[kind, slot, 1:2] = jnp.sum(probs, axis=0, keepdims=True)
         pair_stats[kind, slot, 2:3] = jnp.sum(probs * prob_grad, axis=0, keepdims=True)
 
@@ -236,7 +238,7 @@
 
     def merge(a, b):
         highest = jnp.maximum(a[0], b[0])
-        fa, fb = jnp.exp(a[0] - highest), jnp.exp(b[0] - highest)
+        fa, fb = jnp.exp2(a[0] - highest), jnp.exp2(b[0] - highest)
         return highest, a[1] * fa + b[1] * fb, a[2] * fa + b[2] * fb
 
     def stat_copy(block, target):
@@ -259,11 +261,11 @@
         finish(block, stat(total))
 
     def finish(block, value):
-        fin[block, 0:1] = value[0] + jnp.log(value[1])
+        fin[block, 0:1] = value[0] + jnp.log2(value[1])
         fin[block, 1:2] = value[2] / value[1]
 
     def weights(kind, slot, block):
-        probs = pe[kind, slot] * jnp.exp(pair_stats[kind, slot, 0:1] - fin[block, 0:1])
+        probs = pe[kind, slot] * jnp.exp2(pair_stats[kind, slot, 0:1] - fin[block, 0:1])
         score_grad = (probs * (pd[kind, slot] - fin[block, 1:2])).astype(jnp.bfloat16)
         return probs.astype(jnp.bfloat16), score_grad
 
@@ -557,7 +559,7 @@
 
 def flush(*refs):
     sem = refs[-1]
-    copies = [pltpu.make_async_copy(refs[i], refs[i + 4], sem.at[i]) for i in range(4)]
+    copies = [pltpu.make_async_copy(refs[i], refs[i + 4], sem) for i in range(4)]
     for copy in copies:
         copy.start()
     for copy in copies:
@@ -617,7 +619,7 @@
                 jax.ShapeDtypeStruct(queries.shape, kind) for kind in (bf16, f32, f32, f32)),
             in_specs=[vmem] * 4,
             out_specs=(anywhere,) * 4,
-            scratch_shapes=[dma((4,))],
+            scratch_shapes=[dma],
         )(*(pltpu.with_memory_space_constraint(result, pltpu.VMEM) for result in results))
 
     spec = P(("dp", "ctx"), None)

time: 20.8 us -> 20.7 us (level)
  no operation moved by 1% of the time
where the time goes in v5:
time: 20.7 us; the launch traced here: 20.6 us
  Pallas kernels  19.9 us (96%)
  between operations  0.64 us (3%)
    pallas_call x1, Pallas kernels, local(): pl.pallas_call(functools.partial(kernel, n, rows), out_shape=tuple((pltpu...  19.2 us
    pallas_call x1, Pallas kernels, local(): pl.pallas_call(flush, out_shape=tuple((jax.ShapeDtypeStruct(queries.shape...  0.79 us

profile of v5, /device:TPU:0, one launch (start us, length us, event | category | flops | bytes accessed | tf_op | source)
XLA Modules:
  0.0 20.6 jit_solution(4284832728068883886)
XLA Ops:
  0.6 19.2 %shard_map.84 = (bf16[144,256]{1,0:T(8,128)(2,1)S(1)}, f32[144,256]{1,0:T(8,128)S(1)}, f32[144,256]{1,0:T(8,128)S(1)}, f32[144,256]{1,0:T(8,128)S(1)}) custom-call(bf16[144,256]{1,0:T(8,128)(2,1)} %q_in.1, bf16[144,256]{1,0:T(8,128)(2,1)} %k_in.1, bf16[144,256]{1,0:T(8,128)(2,1)} %v_in.1, bf16[144,256]{1,0:T(8,128)(2,1)} %g_in.1, s32[1,144]{1,0:T(1,128)} %bitcast.1), custom_call_target="tpu_custom_call" | custom-call | tf_op jit(solution)/shard_map/pallas_call | solution.py:579
  19.8 0.8 %shard_map.85 = (bf16[144,256]{1,0:T(8,128)(2,1)}, f32[144,256]{1,0:T(8,128)}, f32[144,256]{1,0:T(8,128)}, f32[144,256]{1,0:T(8,128)}) custom-call(bf16[144,256]{1,0:T(8,128)(2,1)S(1)} %get-tuple-element.8.refs_0_, f32[144,256]{1,0:T(8,128)S(1)} %get-tuple-element.9.refs_1_, f32[144,256]{1,0:T(8,128)S(1)} %get-tuple-element.10.refs_2_, ...), custom_call_target="tpu_custom_call" | custom-call | tf_op jit(solution)/shard_map/pallas_call | solution.py:616

commit v6 on v5

--- a/solution.py
+++ b/solution.py
@@ -391,12 +391,13 @@
         key_side(1, 1, 1, alt.at[0], alt.at[1])
         settle(last)
         far, far_grad = weights(1, last, last)
-        ret_out[0] = (alt[0] + dot(far, buf[GRAD, last], 1, 0)).astype(jnp.bfloat16)
-        ret_copy(HUB, DV, 0, 0, 0).start()
-        ret_out[1] = ((alt[1] + dot(far_grad, buf[QUERY, last], 1, 0)) * scaling).astype(jnp.bfloat16)
-        ret_copy(HUB, DK, 1, 0, 0).start()
-        ret_copy(HUB, DV, 0, 0, 1).start()
-        ret_copy(HUB, DK, 1, 0, 1).start()
+        for portion in range(HEADS):
+            part = slice(portion * rows, (portion + 1) * rows)
+            ret_out[0, part] = (alt[0, part] + dot(far[part], buf[GRAD, last], 1, 0)).astype(jnp.bfloat16)
+            ret_copy(HUB, DV, 0, 0, portion).start()
+            ret_out[1, part] = (
+                (alt[1, part] + dot(far_grad[part], buf[QUERY, last], 1, 0)) * scaling).astype(jnp.bfloat16)
+            ret_copy(HUB, DK, 1, 0, portion).start()
         near, near_grad = weights(0, last, last)
         output, query_grad = query_side(far, far_grad, near, near_grad)
         send_back(HUB, OUT, 2 * last, last, output)

time: 20.7 us -> 20.7 us (level)
  no operation moved by 1% of the time
where the time goes in v6:
time: 20.7 us; the launch traced here: 20.6 us
  Pallas kernels  19.9 us (96%)
  between operations  0.64 us (3%)
    pallas_call x1, Pallas kernels, local(): pl.pallas_call(functools.partial(kernel, n, rows), out_shape=tuple((pltpu...  19.1 us
    pallas_call x1, Pallas kernels, local(): pl.pallas_call(flush, out_shape=tuple((jax.ShapeDtypeStruct(queries.shape...  0.79 us

profile of v6, /device:TPU:0, one launch (start us, length us, event | category | flops | bytes accessed | tf_op | source)
XLA Modules:
  0.0 20.6 jit_solution(7160325428198156087)
XLA Ops:
  0.6 19.1 %shard_map.84 = (bf16[144,256]{1,0:T(8,128)(2,1)S(1)}, f32[144,256]{1,0:T(8,128)S(1)}, f32[144,256]{1,0:T(8,128)S(1)}, f32[144,256]{1,0:T(8,128)S(1)}) custom-call(bf16[144,256]{1,0:T(8,128)(2,1)} %q_in.1, bf16[144,256]{1,0:T(8,128)(2,1)} %k_in.1, bf16[144,256]{1,0:T(8,128)(2,1)} %v_in.1, bf16[144,256]{1,0:T(8,128)(2,1)} %g_in.1, s32[1,144]{1,0:T(1,128)} %bitcast.1), custom_call_target="tpu_custom_call" | custom-call | tf_op jit(solution)/shard_map/pallas_call | solution.py:580
  19.8 0.8 %shard_map.85 = (bf16[144,256]{1,0:T(8,128)(2,1)}, f32[144,256]{1,0:T(8,128)}, f32[144,256]{1,0:T(8,128)}, f32[144,256]{1,0:T(8,128)}) custom-call(bf16[144,256]{1,0:T(8,128)(2,1)S(1)} %get-tuple-element.8.refs_0_, f32[144,256]{1,0:T(8,128)S(1)} %get-tuple-element.9.refs_1_, f32[144,256]{1,0:T(8,128)S(1)} %get-tuple-element.10.refs_2_, ...), custom_call_target="tpu_custom_call" | custom-call | tf_op jit(solution)/shard_map/pallas_call | solution.py:617
